TPU v7x, 32 devices: a whole 2x2x4 slice. The times are simulated.
32 devices in a mesh: gx: 2 (over y), gy: 4 (over x, core), gz: 4 (over z).
Axes of the slice: x: 2, y: 2, z: 4, core: 2. Of those that a mesh axis runs over, the one named last changes fastest.
Arguments:
- snapshots: bfloat16 [16, 64, 64, 256], P('gx', 'gy', 'gz'), may hold values from -1500 to 1500
- sketch: float32 [256, 256], replicated, may hold values from -0.5 to 1.5
- velocity: float32 [3, 16, 64, 64], P(None, 'gx', 'gy', 'gz'), may hold values from -4 to 4
- viscosity: float32 [16, 64, 64], P('gx', 'gy', 'gz'), may hold values from 0.2 to 2
Outputs:
- applied_modes: bfloat16 [16, 64, 64, 256], P('gx', 'gy', 'gz')
- reduced: float32 [256, 256], replicated
All inputs are finite; a program needn't handle non-finite values.
Results may differ from a plain program's by a relative error of at most 0.0015.
The roundings to bfloat16 on the way count: a program that leaves them out, or rounds other values in their place, can miss the bound.
Values may be sent and summed in bfloat16 or wider, within the bound.
No kernel may reach another device: no remote copies, remote signals or barrier semaphores. Data moves between devices by JAX's collectives and lax.ppermute only.
A program may use at most 64 MiB of HBM per device.

v0:
```python
import jax
import jax.numpy as jnp
from jax import lax
from jax.sharding import PartitionSpec as P


def padded_2(cells, sides, width):
    for axis, dim in sides:
        count = lax.axis_size(axis)
        ends = count - 1
        head = lax.slice_in_dim(cells, 0, width, axis=dim)
        tail = lax.slice_in_dim(cells, cells.shape[dim] - width, cells.shape[dim], axis=dim)
        cells = jnp.concatenate(
            [
                lax.ppermute(tail, axis, [(i, (i + 1) % count) for i in range(ends)]),
                cells,
                lax.ppermute(head, axis, [((i + 1) % count, i) for i in range(ends)]),
            ],
            axis=dim,
        )
    return cells


def apply_operator(padded, velocity, viscosity):
    centre = padded[1:-1, 1:-1, 1:-1]
    east_side = padded[2:, 1:-1, 1:-1]
    west_side = padded[:-2, 1:-1, 1:-1]
    north_side = padded[1:-1, 2:, 1:-1]
    south_side = padded[1:-1, :-2, 1:-1]
    upper_side = padded[1:-1, 1:-1, 2:]
    lower_side = padded[1:-1, 1:-1, :-2]
    neighbours = east_side + west_side + north_side + south_side + upper_side + lower_side
    viscous_term = viscosity[..., None] * (6.0 * centre - neighbours)
    flow_term = velocity[0][..., None] * (east_side - west_side)
    flow_term = flow_term + velocity[1][..., None] * (north_side - south_side)
    flow_term = flow_term + velocity[2][..., None] * (upper_side - lower_side)
    return viscous_term + 0.5 * flow_term


def inner_rows(left_rows, right_rows, precision):
    return lax.dot_general(
        left_rows,
        right_rows,
        (((0,), (0,)), ((), ())),
        precision=precision,
        preferred_element_type=jnp.float32,
    )


def per_device(snapshots, sketch, velocity, viscosity):
    highest = lax.Precision.HIGHEST
    columns = sketch.shape[0]
    cells_x, cells_y, cells_z = (snapshots.shape[0], snapshots.shape[1], snapshots.shape[2])
    ncells = (
        cells_x
        * cells_y
        * cells_z
        * lax.axis_size("gx")
        * lax.axis_size("gy")
        * lax.axis_size("gz")
    )
    sketched = jnp.dot(
        snapshots.reshape(-1, columns).astype(jnp.float32), sketch, precision=highest
    ).astype(jnp.bfloat16)
    local_gram = inner_rows(sketched, sketched, None) / ncells
    gram_matrix = lax.psum(local_gram, ("gx", "gy", "gz"))
    lower_factor = jnp.linalg.cholesky(gram_matrix)
    inverse = jax.scipy.linalg.solve_triangular(
        lower_factor, jnp.eye(columns, dtype=jnp.float32), lower=True
    )
    mode_rows = jnp.dot(sketched.astype(jnp.float32), inverse.T, precision=highest)
    mode_field = mode_rows.reshape(cells_x, cells_y, cells_z, columns)
    padded_modes = padded_2(mode_field, (("gx", 0), ("gy", 1), ("gz", 2)), 1)
    image_rows = apply_operator(padded_modes, velocity, viscosity).reshape(-1, columns)
    local_reduced = inner_rows(mode_rows, image_rows, highest) / ncells
    reduced = lax.psum(local_reduced, ("gx", "gy", "gz"))
    applied_modes = image_rows.reshape(cells_x, cells_y, cells_z, columns).astype(jnp.bfloat16)
    return (applied_modes, reduced)


def solution(mesh):
    in_specs = (P("gx", "gy", "gz", None), P(), P(None, "gx", "gy", "gz"), P("gx", "gy", "gz"))
    out_specs = (P("gx", "gy", "gz", None), P())
    return jax.shard_map(
        per_device, mesh=mesh, in_specs=in_specs, out_specs=out_specs, check_vma=False
    )
```

profile of v0, /device:TPU:0, one launch (start us, length us, event | category | flops | bytes accessed | tf_op | source)
XLA Modules:
  0.0 380.9 jit_solution(7893172982498539869)
XLA Ops:
  8.4 2.0 convolution_convert_fusion
  10.4 1.2 convolution_multiply_fusion.1
  11.7 131.6 %all-reduce.4.cloned.1.call-done = f32[256,256]{0,1:T(8,128)} async-done(((f32[256,256]{0,1:T(8,128)}), f32[256,256]{0,1:T(8,128)}) %all-reduce.4.cloned.1.call-update) | async-done | bytes 262160 | tf_op jit(solution)/shard_map/psum | solution.py:66
  145.4 11.7 %cholesky.50 = f32[128,128]{1,0:T(8,128)S(1)} custom-call(f32[128,128]{1,0:T(8,128)S(1)} %cholesky.118), custom_call_target="Cholesky" | custom-call | tf_op jit(solution)/shard_map/jit(cholesky)/cholesky | solution.py:67
  157.2 9.8 %custom-call.15 = f32[1,128,128]{1,2,0:T(8,128)S(1)} custom-call(f32[1,128,128]{2,1,0:T(8,128)S(1)} %get-tuple-element.36), custom_call_target="InvertDiagBlocksLowerTriangular" | custom-call | tf_op jit(solution)/shard_map/jit(cholesky)/cholesky | solution.py:67
  167.5 11.7 %cholesky.105 = f32[128,128]{1,0:T(8,128)S(1)} custom-call(f32[128,128]{1,0:T(8,128)S(1)} %convolution_subtract_fusion.1), custom_call_target="Cholesky" | custom-call | tf_op jit(solution)/shard_map/jit(cholesky)/cholesky | solution.py:67
  181.4 4.2 %while.1 = (s32[]{:T(128)}, f32[256,256]{1,0:T(8,128)S(1)}, s32[2,2]{1,0:T(2,128)S(1)}, f32[2,128,128]{2,1,0:T(8,128)S(1)}, s32[]{:T(128)}) while((s32[]{:T(128)}, f32[256,256]{1,0:T(8,128)S(1)}, s32[2,2]{1,0:T(2,128)S(1)}, f32[2,128,128]{2,1,0:T(8,128)S(1)}, s32[]{:T(128)}) %tuple.34), condition=%wide.while_cond, body=%wide.while_body.sunk | while | flops 2 | bytes 131189 | solution.py:68
  182.1 1.4 bitcast_dynamic-update-slice_fusion.2
  184.2 1.4 bitcast_dynamic-update-slice_fusion.2
  185.6 19.7 %custom-call.16 = f32[2,128,128]{1,2,0:T(8,128)S(1)} custom-call(f32[2,128,128]{2,1,0:T(8,128)S(1)} %get-tuple-element.9), custom_call_target="InvertDiagBlocksLowerTriangular" | custom-call | tf_op jit(solution)/shard_map/jit(_solve_triangular)/triangular_solve | solution.py:68
  207.2 1.3 collective-permute-start
  208.5 4.6 %collective-permute-start.1 = (f32[1,16,16,256]{3,2,1,0:T(8,128)S(1)}, f32[1,16,16,256]{3,2,1,0:T(8,128)S(1)}, u32[]{:S(2)}, u32[]{:S(2)}) collective-permute-start(f32[1,16,16,256]{3,2,1,0:T(8,128)S(1)} %bitcast.54), channel_id=1, source_target_pairs={{0,16},{1,17},{2,18},{3,19},{4,20},{5,21},{6,22},{7,23},{8,24},{9,... | collective-permute-start | bytes 786440 | tf_op jit(solution)/shard_map/ppermute | solution.py:15
  213.1 3.3 collective-permute-done
  217.6 1.4 collective-permute-start.3
  219.1 1.3 collective-permute-start.2
  220.4 3.7 collective-permute-done.2
  224.3 1.3 collective-permute-start.4
  225.6 4.6 %collective-permute-start.5 = (f32[10,18,1,256]{3,2,1,0:T(1,128)S(1)}, f32[10,18,1,256]{3,2,1,0:T(1,128)S(1)}, u32[]{:S(2)}, u32[]{:S(2)}) collective-permute-start(f32[10,18,1,256]{3,2,1,0:T(1,128)S(1)} %get-tuple-element.25), channel_id=1, source_target_pairs={{0,1},{1,2},{2,3},{4,5},{5,6},{6,7},{8,9},{9,10},{10,11},{12,13},{... | collective-permute-start | bytes 552968 | tf_op jit(solution)/shard_map/ppermute | solution.py:15
  230.2 1.5 collective-permute-done.4
  231.7 1.5 collective-permute-done.5
  233.2 4.6 %fusion.13 = (bf16[8,16,16,256]{3,2,1,0:T(8,128)(2,1)}, f32[8,16,16,256]{3,2,1,0:T(8,128)S(1)}) fusion(f32[8,16,16]{2,1,0:T(8,128)S(1)} %get-tuple-element.31, f32[8,16,16]{2,1,0:T(8,128)S(1)} %get-tuple-element.32, f32[8,16,16]{2,1,0:T(8,128)S(1)} %get-tuple-element.30, f32[10,1,16,256]{3,2,1,0:T(8,128)S(1)} %collective-permute-done.2, ...), kind=kLoop, calls=%fused_computation.66 | loop fusion | flops 19398656 | bytes 6496256 | tf_op jit(solution)/shard_map/convert_element_type | solution.py:77
  237.8 4.3 %convolution_multiply_fusion = f32[256,256]{0,1:T(8,128)} fusion(f32[2048,256]{1,0:T(8,128)S(1)} %fusion, f32[2048,256]{1,0:T(8,128)S(1)} %bitcast.53), kind=kOutput, calls=%fused_computation.22 | convolution fusion | flops 1610678272 | bytes 4456448 | tf_op jit(solution)/shard_map/dot_general | solution.py:41
  242.1 130.2 %all-reduce.6.cloned.1.call-done = f32[256,256]{0,1:T(8,128)} async-done(((f32[256,256]{0,1:T(8,128)}), f32[256,256]{0,1:T(8,128)}) %all-reduce.6.cloned.1.call-update) | async-done | bytes 262160 | tf_op jit(solution)/shard_map/psum | solution.py:76
  372.3 1.8 copy.9
  (38 shorter events, 9.4 us)
Async XLA Ops:
  7.2 1.2 copy-start
  7.2 136.1 %all-reduce.4.cloned.1.call-start = ((), (), s32[]{:S(2)}) async-start(), calls=%async_computation | async-start | bytes 524288 | tf_op jit(solution)/shard_map/psum | solution.py:66
  11.6 360.7 %all-reduce.6.cloned.1.call-start = ((), (), s32[]{:S(2)}) async-start(), calls=%async_computation.1 | async-start | bytes 524288 | tf_op jit(solution)/shard_map/psum | solution.py:76
  207.2 9.1 %collective-permute-start = (f32[1,16,16,256]{3,2,1,0:T(8,128)S(1)}, f32[1,16,16,256]{3,2,1,0:T(8,128)S(1)}, u32[]{:S(2)}, u32[]{:S(2)}) collective-permute-start(f32[1,16,16,256]{3,2,1,0:T(8,128)S(1)} %bitcast.55), channel_id=1, source_target_pairs={{16,0},{17,1},{18,2},{19,3},{20,4},{21,5},{22,6},{23,7},{24,8},{25... | collective-permute-start | bytes 786440 | tf_op jit(solution)/shard_map/ppermute | solution.py:17
  208.5 9.0 %collective-permute-start.1 = (f32[1,16,16,256]{3,2,1,0:T(8,128)S(1)}, f32[1,16,16,256]{3,2,1,0:T(8,128)S(1)}, u32[]{:S(2)}, u32[]{:S(2)}) collective-permute-start(f32[1,16,16,256]{3,2,1,0:T(8,128)S(1)} %bitcast.54), channel_id=1, source_target_pairs={{0,16},{1,17},{2,18},{3,19},{4,20},{5,21},{6,22},{7,23},{8,24},{9,... | collective-permute-start | bytes 786440 | tf_op jit(solution)/shard_map/ppermute | solution.py:15
  217.6 12.6 %copy-start.1 = (f32[3,8,16,16]{3,2,1,0:T(8,128)S(1)}, f32[3,8,16,16]{3,2,1,0:T(8,128)}, u32[]{:S(2)}) copy-start(f32[3,8,16,16]{3,2,1,0:T(8,128)} %param.6) | copy-start | bytes 73732
  217.6 15.6 %copy-start.2 = (f32[8,16,16]{2,1,0:T(8,128)S(1)}, f32[8,16,16]{2,1,0:T(8,128)}, u32[]{:S(2)}) copy-start(f32[8,16,16]{2,1,0:T(8,128)} %param.7) | copy-start | bytes 24580
  217.6 2.7 collective-permute-start.3
  219.1 5.0 %collective-permute-start.2 = (f32[10,1,16,256]{3,2,1,0:T(8,128)S(1)}, f32[10,1,16,256]{3,2,1,0:T(8,128)S(1)}, u32[]{:S(2)}, u32[]{:S(2)}) collective-permute-start(f32[10,1,16,256]{3,2,1,0:T(8,128)S(1)} %get-tuple-element.27), channel_id=1, source_target_pairs={{4,0},{8,4},{12,8},{5,1},{9,5},{13,9},{6,2},{10,6},{14,10},{7,3},{... | collective-permute-start | bytes 491528 | tf_op jit(solution)/shard_map/ppermute | solution.py:17
  224.3 7.4 %collective-permute-start.4 = (f32[10,18,1,256]{3,2,1,0:T(1,128)S(1)}, f32[10,18,1,256]{3,2,1,0:T(1,128)S(1)}, u32[]{:S(2)}, u32[]{:S(2)}) collective-permute-start(f32[10,18,1,256]{3,2,1,0:T(1,128)S(1)} %get-tuple-element.24), channel_id=1, source_target_pairs={{1,0},{2,1},{3,2},{5,4},{6,5},{7,6},{9,8},{10,9},{11,10},{13,12},{... | collective-permute-start | bytes 552968 | tf_op jit(solution)/shard_map/ppermute | solution.py:17
  225.6 7.6 %collective-permute-start.5 = (f32[10,18,1,256]{3,2,1,0:T(1,128)S(1)}, f32[10,18,1,256]{3,2,1,0:T(1,128)S(1)}, u32[]{:S(2)}, u32[]{:S(2)}) collective-permute-start(f32[10,18,1,256]{3,2,1,0:T(1,128)S(1)} %get-tuple-element.25), channel_id=1, source_target_pairs={{0,1},{1,2},{2,3},{4,5},{5,6},{6,7},{8,9},{9,10},{10,11},{12,13},{... | collective-permute-start | bytes 552968 | tf_op jit(solution)/shard_map/ppermute | solution.py:15
Sparse Core Ops, SparseCore 0:
  14.1 129.2 all-reduce.3
  242.2 130.0 all-reduce.5
where the time goes:
time: 381 us
  waiting for transfers between devices  273 us (72%)
  other arithmetic  59.6 us (16%)
  between operations  15.6 us (4%)
  starting transfers between devices  14.5 us (4%)
  matrix products  9.81 us (3%)
  local copies, waits for them, and re-layouts  8.22 us (2%)
    psum x1, waiting for transfers between devices, per_device(): gram_matrix = lax.psum(local_gram, ('gx', 'gy', 'gz'))  132 us
    psum x1, waiting for transfers between devices, per_device(): reduced = lax.psum(local_reduced, ('gx', 'gy', 'gz'))  130 us
    another operation x6, other arithmetic, per_device(): lower_factor = jnp.linalg.cholesky(gram_matrix)  34 us
    another operation x3, other arithmetic, per_device(): jax.scipy.linalg.solve_triangular(lower_factor, jnp.eye(columns, dtype=jn...  19.7 us
    ppermute x3, starting transfers between devices, padded_2(): lax.ppermute(tail, axis, [(i, (i + 1) % count) for i in range(ends)])  10.6 us
    ppermute x3, waiting for transfers between devices, padded_2(): lax.ppermute(head, axis, [((i + 1) % count, i) for i in range(ends)])  8.48 us
  transfers between devices with their start and end apart: 8, of which 7 were waited for; matrix products, arithmetic and copies ran while one was open for 0% of the time, Pallas kernels for 0%

commit v1 on v0

--- a/solution.py
+++ b/solution.py
@@ -73,7 +73,8 @@
     padded_modes = padded_2(mode_field, (("gx", 0), ("gy", 1), ("gz", 2)), 1)
     image_rows = apply_operator(padded_modes, velocity, viscosity).reshape(-1, columns)
     local_reduced = inner_rows(mode_rows, image_rows, highest) / ncells
-    reduced = lax.psum(local_reduced, ("gx", "gy", "gz"))
+    parts = lax.all_gather(local_reduced, ("gx", "gy", "gz"), axis=0, tiled=False)
+    reduced = parts.sum(axis=0)
     applied_modes = image_rows.reshape(cells_x, cells_y, cells_z, columns).astype(jnp.bfloat16)
     return (applied_modes, reduced)
 

time: 381 us -> 347 us (0.911)
  waiting for transfers between devices: 273 us -> 230 us
  local copies, waits for them, and re-layouts: 8.22 us -> 14.1 us
    psum x1 -> x0, waiting for transfers between devices: 130 us -> none  [per_device(): reduced = lax.psum(local_reduced, ('gx', 'gy', 'gz'))]
    all_gather x0 -> x1, waiting for transfers between devices: none -> 87.7 us  [per_device(): lax.all_gather(local_reduced, ('gx', 'gy', 'gz'), axis=0, tiled=False)]
    unnamed x7 -> x8, local copies, waits for them, and re-layouts: 2.97 us -> 8.86 us
where the time goes in v1:
time: 347 us; the launch traced here: 346 us
  waiting for transfers between devices  230 us (66%)
  other arithmetic  61.5 us (18%)
  between operations  15.6 us (4%)
  starting transfers between devices  14.5 us (4%)
  local copies, waits for them, and re-layouts  14.1 us (4%)
  matrix products  9.81 us (3%)
    psum x1, waiting for transfers between devices, per_device(): gram_matrix = lax.psum(local_gram, ('gx', 'gy', 'gz'))  132 us
    all_gather x1, waiting for transfers between devices, per_device(): lax.all_gather(local_reduced, ('gx', 'gy', 'gz'), axis=0, tiled=False)  87.7 us
    another operation x6, other arithmetic, per_device(): lower_factor = jnp.linalg.cholesky(gram_matrix)  34 us
    another operation x3, other arithmetic, per_device(): jax.scipy.linalg.solve_triangular(lower_factor, jnp.eye(columns, dtype=jn...  19.7 us
    ppermute x3, starting transfers between devices, padded_2(): lax.ppermute(tail, axis, [(i, (i + 1) % count) for i in range(ends)])  10.6 us
    unnamed x8, local copies, waits for them, and re-layouts  8.86 us
    ppermute x3, waiting for transfers between devices, padded_2(): lax.ppermute(head, axis, [((i + 1) % count, i) for i in range(ends)])  8.48 us
  transfers between devices with their start and end apart: 8, of which 7 were waited for; matrix products, arithmetic and copies ran while one was open for 0% of the time, Pallas kernels for 0%

profile of v1, /device:TPU:0, one launch (start us, length us, event | category | flops | bytes accessed | tf_op | source)
XLA Modules:
  0.0 346.2 jit_solution(11412699703965742877)
XLA Ops:
  8.4 2.0 convolution_convert_fusion
  11.7 131.6 %all-reduce.3.cloned.1.call-done = f32[256,256]{0,1:T(8,128)} async-done(((f32[256,256]{0,1:T(8,128)}), f32[256,256]{0,1:T(8,128)}) %all-reduce.3.cloned.1.call-update) | async-done | bytes 262160 | tf_op jit(solution)/shard_map/psum | solution.py:66
  145.4 11.7 %cholesky.50 = f32[128,128]{1,0:T(8,128)S(1)} custom-call(f32[128,128]{1,0:T(8,128)S(1)} %cholesky.118), custom_call_target="Cholesky" | custom-call | tf_op jit(solution)/shard_map/jit(cholesky)/cholesky | solution.py:67
  157.2 9.8 %custom-call.15 = f32[1,128,128]{1,2,0:T(8,128)S(1)} custom-call(f32[1,128,128]{2,1,0:T(8,128)S(1)} %get-tuple-element.36), custom_call_target="InvertDiagBlocksLowerTriangular" | custom-call | tf_op jit(solution)/shard_map/jit(cholesky)/cholesky | solution.py:67
  167.5 11.7 %cholesky.105 = f32[128,128]{1,0:T(8,128)S(1)} custom-call(f32[128,128]{1,0:T(8,128)S(1)} %convolution_subtract_fusion.1), custom_call_target="Cholesky" | custom-call | tf_op jit(solution)/shard_map/jit(cholesky)/cholesky | solution.py:67
  181.4 4.2 %while.1 = (s32[]{:T(128)}, f32[256,256]{1,0:T(8,128)S(1)}, s32[2,2]{1,0:T(2,128)S(1)}, f32[2,128,128]{2,1,0:T(8,128)S(1)}, s32[]{:T(128)}) while((s32[]{:T(128)}, f32[256,256]{1,0:T(8,128)S(1)}, s32[2,2]{1,0:T(2,128)S(1)}, f32[2,128,128]{2,1,0:T(8,128)S(1)}, s32[]{:T(128)}) %tuple.34), condition=%wide.while_cond, body=%wide.while_body.sunk | while | flops 2 | bytes 131189 | solution.py:68
  182.1 1.4 bitcast_dynamic-update-slice_fusion.2
  184.2 1.4 bitcast_dynamic-update-slice_fusion.2
  185.6 19.7 %custom-call.16 = f32[2,128,128]{1,2,0:T(8,128)S(1)} custom-call(f32[2,128,128]{2,1,0:T(8,128)S(1)} %get-tuple-element.9), custom_call_target="InvertDiagBlocksLowerTriangular" | custom-call | tf_op jit(solution)/shard_map/jit(_solve_triangular)/triangular_solve | solution.py:68
  207.2 1.3 collective-permute-start
  208.5 4.6 %collective-permute-start.1 = (f32[1,16,16,256]{3,2,1,0:T(8,128)S(1)}, f32[1,16,16,256]{3,2,1,0:T(8,128)S(1)}, u32[]{:S(2)}, u32[]{:S(2)}) collective-permute-start(f32[1,16,16,256]{3,2,1,0:T(8,128)S(1)} %bitcast.60), channel_id=1, source_target_pairs={{0,16},{1,17},{2,18},{3,19},{4,20},{5,21},{6,22},{7,23},{8,24},{9,... | collective-permute-start | bytes 786440 | tf_op jit(solution)/shard_map/ppermute | solution.py:15
  213.1 3.3 collective-permute-done
  217.6 1.4 collective-permute-start.3
  219.1 1.3 collective-permute-start.2
  220.4 3.7 %collective-permute-done.2 = f32[10,1,16,256]{3,2,1,0:T(8,128)S(1)} collective-permute-done((f32[10,1,16,256]{3,2,1,0:T(8,128)S(1)}, f32[10,1,16,256]{3,2,1,0:T(8,128)S(1)}, u32[]{:S(2)}, u32[]{:S(2)}) %collective-permute-start.2) | collective-permute-done | bytes 163872 | tf_op jit(solution)/shard_map/ppermute | solution.py:17
  224.3 1.3 collective-permute-start.4
  225.6 4.6 %collective-permute-start.5 = (f32[10,18,1,256]{3,2,1,0:T(1,128)S(1)}, f32[10,18,1,256]{3,2,1,0:T(1,128)S(1)}, u32[]{:S(2)}, u32[]{:S(2)}) collective-permute-start(f32[10,18,1,256]{3,2,1,0:T(1,128)S(1)} %get-tuple-element.25), channel_id=1, source_target_pairs={{0,1},{1,2},{2,3},{4,5},{5,6},{6,7},{8,9},{9,10},{10,11},{12,13},{... | collective-permute-start | bytes 552968 | tf_op jit(solution)/shard_map/ppermute | solution.py:15
  230.2 1.5 collective-permute-done.4
  231.7 1.5 collective-permute-done.5
  233.2 4.6 %fusion.13 = (bf16[8,16,16,256]{3,2,1,0:T(8,128)(2,1)}, f32[8,16,16,256]{3,2,1,0:T(8,128)S(1)}) fusion(f32[8,16,16]{2,1,0:T(8,128)S(1)} %get-tuple-element.31, f32[8,16,16]{2,1,0:T(8,128)S(1)} %get-tuple-element.32, f32[8,16,16]{2,1,0:T(8,128)S(1)} %get-tuple-element.30, f32[10,1,16,256]{3,2,1,0:T(8,128)S(1)} %collective-permute-done.2, ...), kind=kLoop, calls=%fused_computation.67 | loop fusion | flops 19398656 | bytes 6496256 | tf_op jit(solution)/shard_map/convert_element_type | solution.py:78
  237.8 4.3 %convolution_multiply_fusion = f32[256,256]{0,1:T(8,128)} fusion(f32[2048,256]{1,0:T(8,128)S(1)} %fusion, f32[2048,256]{1,0:T(8,128)S(1)} %bitcast.59), kind=kOutput, calls=%fused_computation.23 | convolution fusion | flops 1610678272 | bytes 4456448 | tf_op jit(solution)/shard_map/dot_general | solution.py:41
  242.1 87.7 %all-gather.3.cloned.1.call-done = f32[8192,256]{0,1:T(8,128)} async-done(((f32[256,256]{0,1:T(8,128)}), f32[8192,256]{0,1:T(8,128)}) %all-gather.3.cloned.1.call-update) | async-done | bytes 8388624 | tf_op jit(solution)/shard_map/all_gather | solution.py:76
  329.8 6.8 %copy.15 = f32[32,8,32,256]{3,2,1,0:T(8,128)S(1)} copy(f32[32,8,32,256]{3,1,2,0:T(8,128)} %bitcast.58) | data formatting | bytes 16777216
  336.6 1.9 bitcast_reduce_fusion
  (40 shorter events, 11.4 us)
Async XLA Ops:
  7.2 1.2 copy-start
  7.2 136.1 %all-reduce.3.cloned.1.call-start = ((), (), s32[]{:S(2)}) async-start(), calls=%async_computation | async-start | bytes 524288 | tf_op jit(solution)/shard_map/psum | solution.py:66
  11.6 318.2 %all-gather.3.cloned.1.call-start = ((), (), s32[]{:S(2)}) async-start(), calls=%async_computation.1 | async-start | bytes 8650752 | tf_op jit(solution)/shard_map/all_gather | solution.py:76
  207.2 9.1 %collective-permute-start = (f32[1,16,16,256]{3,2,1,0:T(8,128)S(1)}, f32[1,16,16,256]{3,2,1,0:T(8,128)S(1)}, u32[]{:S(2)}, u32[]{:S(2)}) collective-permute-start(f32[1,16,16,256]{3,2,1,0:T(8,128)S(1)} %bitcast.61), channel_id=1, source_target_pairs={{16,0},{17,1},{18,2},{19,3},{20,4},{21,5},{22,6},{23,7},{24,8},{25... | collective-permute-start | bytes 786440 | tf_op jit(solution)/shard_map/ppermute | solution.py:17
  208.5 9.0 %collective-permute-start.1 = (f32[1,16,16,256]{3,2,1,0:T(8,128)S(1)}, f32[1,16,16,256]{3,2,1,0:T(8,128)S(1)}, u32[]{:S(2)}, u32[]{:S(2)}) collective-permute-start(f32[1,16,16,256]{3,2,1,0:T(8,128)S(1)} %bitcast.60), channel_id=1, source_target_pairs={{0,16},{1,17},{2,18},{3,19},{4,20},{5,21},{6,22},{7,23},{8,24},{9,... | collective-permute-start | bytes 786440 | tf_op jit(solution)/shard_map/ppermute | solution.py:15
  217.6 12.6 %copy-start.1 = (f32[3,8,16,16]{3,2,1,0:T(8,128)S(1)}, f32[3,8,16,16]{3,2,1,0:T(8,128)}, u32[]{:S(2)}) copy-start(f32[3,8,16,16]{3,2,1,0:T(8,128)} %param.6) | copy-start | bytes 73732
  217.6 15.6 %copy-start.2 = (f32[8,16,16]{2,1,0:T(8,128)S(1)}, f32[8,16,16]{2,1,0:T(8,128)}, u32[]{:S(2)}) copy-start(f32[8,16,16]{2,1,0:T(8,128)} %param.7) | copy-start | bytes 24580
  217.6 2.7 collective-permute-start.3
  219.1 5.0 %collective-permute-start.2 = (f32[10,1,16,256]{3,2,1,0:T(8,128)S(1)}, f32[10,1,16,256]{3,2,1,0:T(8,128)S(1)}, u32[]{:S(2)}, u32[]{:S(2)}) collective-permute-start(f32[10,1,16,256]{3,2,1,0:T(8,128)S(1)} %get-tuple-element.27), channel_id=1, source_target_pairs={{4,0},{8,4},{12,8},{5,1},{9,5},{13,9},{6,2},{10,6},{14,10},{7,3},{... | collective-permute-start | bytes 491528 | tf_op jit(solution)/shard_map/ppermute | solution.py:17
  224.3 7.4 %collective-permute-start.4 = (f32[10,18,1,256]{3,2,1,0:T(1,128)S(1)}, f32[10,18,1,256]{3,2,1,0:T(1,128)S(1)}, u32[]{:S(2)}, u32[]{:S(2)}) collective-permute-start(f32[10,18,1,256]{3,2,1,0:T(1,128)S(1)} %get-tuple-element.24), channel_id=1, source_target_pairs={{1,0},{2,1},{3,2},{5,4},{6,5},{7,6},{9,8},{10,9},{11,10},{13,12},{... | collective-permute-start | bytes 552968 | tf_op jit(solution)/shard_map/ppermute | solution.py:17
  225.6 7.6 %collective-permute-start.5 = (f32[10,18,1,256]{3,2,1,0:T(1,128)S(1)}, f32[10,18,1,256]{3,2,1,0:T(1,128)S(1)}, u32[]{:S(2)}, u32[]{:S(2)}) collective-permute-start(f32[10,18,1,256]{3,2,1,0:T(1,128)S(1)} %get-tuple-element.25), channel_id=1, source_target_pairs={{0,1},{1,2},{2,3},{4,5},{5,6},{6,7},{8,9},{9,10},{10,11},{12,13},{... | collective-permute-start | bytes 552968 | tf_op jit(solution)/shard_map/ppermute | solution.py:15
Sparse Core Ops, SparseCore 0:
  14.1 129.2 all-reduce.2
  242.2 87.5 all-gather.2
